TPU v7x, 32 devices: a whole 2x2x4 slice. The times are simulated.
32 devices in a mesh: rep: 4 (over y, x), fsdp: 8 (over z, core).
Axes of the slice: x: 2, y: 2, z: 4, core: 2. Of those that a mesh axis runs over, the one named last changes fastest.
Arguments:
- tokens: float32 [4096, 1024], P(('rep', 'fsdp')), may hold values from -6 to 6
- segment_ids: int32 [4096], replicated, may hold values from 0 to 7, never falling along the last dimension, each value on 1 to 1024 neighbouring positions
- cotangent: float32 [4096, 1024], P(('rep', 'fsdp')), may hold values from -6 to 6
- w_qkv: bfloat16 [1024, 2048], P('fsdp'), may hold values from -0.1875 to 0.1875
- w_out: bfloat16 [1024, 1024], P('fsdp'), may hold values from -0.75 to 0.75
- w_gate_up: bfloat16 [1024, 9216], P('fsdp'), may hold values from -0.1875 to 0.1875
- w_down: bfloat16 [4608, 1024], P('fsdp'), may hold values from -0.09375 to 0.09375
- g_attn: bfloat16 [1024], P('fsdp'), may hold values from 0.099609375 to 1.8984375
- g_query: bfloat16 [64], P('fsdp'), may hold values from 0.099609375 to 1.8984375
- g_key: bfloat16 [64], P('fsdp'), may hold values from 0.099609375 to 1.8984375
- g_ffn: bfloat16 [1024], P('fsdp'), may hold values from 0.099609375 to 1.8984375
Outputs:
- output: float32 [4096, 1024], P(('rep', 'fsdp'))
- grad_tokens: float32 [4096, 1024], P(('rep', 'fsdp'))
- grad_w_qkv: float32 [1024, 2048], P('fsdp')
- grad_w_out: float32 [1024, 1024], P('fsdp')
- grad_w_gate_up: float32 [1024, 9216], P('fsdp')
- grad_w_down: float32 [4608, 1024], P('fsdp')
- grad_g_attn: float32 [1024], P('fsdp')
- grad_g_query: float32 [64], P('fsdp')
- grad_g_key: float32 [64], P('fsdp')
- grad_g_ffn: float32 [1024], P('fsdp')
Inputs may be any that keep to these rules, and one draw needn't show every extreme that they name: `segment_ids`: segment numbers never fall along the tokens; a segment holds 1 to 1024 tokens and one holds exactly 1024.
All inputs are finite; a program needn't handle non-finite values.
Results may differ from a plain program's by a relative error of at most 0.024.
Values may be sent and summed in bfloat16 or wider, within the bound.
A program may use at most 192 MiB of HBM per device.

v0:
```python
import jax
import jax.numpy as jnp
from jax import lax
from jax.sharding import PartitionSpec as P

QUERY_HEADS = 16
KEY_VALUE_HEADS = 8
HEAD_SIZE = 64
FF = 4608
NORM_EPS = 1e-05
ROPE_BASE = 1000000.0
MASK_FILL = -1e30


def rms_forward(values, gain_vec):
    inv_rms = lax.rsqrt(jnp.mean(values * values, axis=-1, keepdims=True) + NORM_EPS)
    return (values * inv_rms * gain_vec, inv_rms)


def root_mean_square_reverse(values, inv_rms, gain_vec, grad_out):
    weighted = grad_out * gain_vec
    grad_values = inv_rms * weighted - values * inv_rms**3 * jnp.mean(
        weighted * values, axis=-1, keepdims=True
    )
    grad_gain = jnp.sum((grad_out * values * inv_rms).reshape(-1, values.shape[-1]), axis=0)
    return (grad_values, grad_gain)


def rope_tables(positions, head_width):
    half_width = head_width // 2
    freqs_base = ROPE_BASE ** (-2.0 * jnp.arange(half_width, dtype=jnp.float32) / head_width)
    angles = positions.astype(jnp.float32)[:, None] * freqs_base[None, :]
    return (jnp.cos(angles)[:, None, :], jnp.sin(angles)[:, None, :])


def rotary_embed_apply(values, rotary_cosine, rotary_sine):
    half_width = values.shape[-1] // 2
    first_half = values[..., :half_width]
    second_half = values[..., half_width:]
    return jnp.concatenate(
        [
            first_half * rotary_cosine - second_half * rotary_sine,
            second_half * rotary_cosine + first_half * rotary_sine,
        ],
        axis=-1,
    )


def rotary_embed_invert(grad_out, rotary_cosine, rotary_sine):
    half_width = grad_out.shape[-1] // 2
    first_half = grad_out[..., :half_width]
    second_half = grad_out[..., half_width:]
    return jnp.concatenate(
        [
            first_half * rotary_cosine + second_half * rotary_sine,
            second_half * rotary_cosine - first_half * rotary_sine,
        ],
        axis=-1,
    )


def score_block(query_lowprec, key_lowprec, attention_mask_matrix):
    scale_dot = query_lowprec.shape[-1] ** (-0.5)
    scores = (
        jnp.einsum("qkgd,tkd->kgqt", query_lowprec, key_lowprec, preferred_element_type=jnp.float32)
        * scale_dot
    )
    return jnp.where(attention_mask_matrix, scores, MASK_FILL)


def attend_forward(query_lowprec, key_lowprec, value_lowprec, attention_mask_matrix):
    scores = score_block(query_lowprec, key_lowprec, attention_mask_matrix)
    top_score = jnp.max(scores, axis=-1, keepdims=True)
    expo_terms = jnp.where(attention_mask_matrix, jnp.exp(scores - top_score), 0.0)
    row_total = jnp.sum(expo_terms, axis=-1, keepdims=True)
    probs = (expo_terms / row_total).astype(jnp.bfloat16)
    mixed = jnp.einsum("kgqt,tkd->qkgd", probs, value_lowprec, preferred_element_type=jnp.float32)
    return (mixed.astype(jnp.bfloat16), top_score + jnp.log(row_total))


def attention_reverse_pass(
    query_lowprec,
    key_lowprec,
    value_lowprec,
    attention_mask_matrix,
    attention_lowprec,
    log_partition_sum,
    grad_attn,
):
    scale_dot = query_lowprec.shape[-1] ** (-0.5)
    scores = score_block(query_lowprec, key_lowprec, attention_mask_matrix)
    probs_again = jnp.where(attention_mask_matrix, jnp.exp(scores - log_partition_sum), 0.0)
    probs_low = probs_again.astype(jnp.bfloat16)
    value_gradient_rows = jnp.einsum(
        "kgqt,qkgd->tkd", probs_low, grad_attn, preferred_element_type=jnp.float32
    )
    d_probs = jnp.einsum(
        "qkgd,tkd->kgqt", grad_attn, value_lowprec, preferred_element_type=jnp.float32
    )
    delta_rows = jnp.sum(
        grad_attn.astype(jnp.float32) * attention_lowprec.astype(jnp.float32), axis=-1
    )
    delta_rows = jnp.transpose(delta_rows, (1, 2, 0))[..., None]
    d_score = (probs_again * (d_probs - delta_rows) * scale_dot).astype(jnp.bfloat16)
    grad_query = jnp.einsum(
        "kgqt,tkd->qkgd", d_score, key_lowprec, preferred_element_type=jnp.float32
    )
    grad_key = jnp.einsum(
        "kgqt,qkgd->tkd", d_score, query_lowprec, preferred_element_type=jnp.float32
    )
    return (grad_query, grad_key, value_gradient_rows)


def tdot(left_arr, right_arr):
    return lax.dot_general(
        left_arr, right_arr, (((0,), (0,)), ((), ())), preferred_element_type=jnp.float32
    )


def transposed_product(left_arr, right_arr):
    return lax.dot_general(
        left_arr, right_arr, (((1,), (1,)), ((), ())), preferred_element_type=jnp.float32
    )


def body(
    tokens, segment_ids, cotangent, w_qkv, w_out, w_gate_up, w_down, g_attn, g_query, g_key, g_ffn
):
    local_rows = tokens.shape[0]
    cluster_size = QUERY_HEADS // KEY_VALUE_HEADS
    seq_devices = lax.axis_size("fsdp")
    cluster_rows = seq_devices * local_rows
    member = lax.axis_index("fsdp")
    own_group = member * local_rows
    group_start = lax.axis_index("rep") * cluster_rows
    own_global = group_start + own_group
    key_value_width = KEY_VALUE_HEADS * HEAD_SIZE
    shards = (w_qkv, w_out, w_gate_up, w_down, g_attn, g_query, g_key, g_ffn)
    collected_rows = (
        lax.all_gather(shards[0], "fsdp", axis=0, tiled=True),
        lax.all_gather(shards[1], "fsdp", axis=0, tiled=True),
        lax.all_gather(shards[2], "fsdp", axis=0, tiled=True),
        lax.all_gather(shards[3], "fsdp", axis=0, tiled=True),
        lax.all_gather(shards[4], "fsdp", axis=0, tiled=True),
        lax.all_gather(shards[5], "fsdp", axis=0, tiled=True),
        lax.all_gather(shards[6], "fsdp", axis=0, tiled=True),
        lax.all_gather(shards[7], "fsdp", axis=0, tiled=True),
    )
    gain_sequence = [gain_arr.astype(jnp.float32) for gain_arr in collected_rows[4:]]
    query_seg = lax.dynamic_slice_in_dim(segment_ids, own_global, local_rows)
    key_seg = lax.dynamic_slice_in_dim(segment_ids, group_start, cluster_rows)
    query_pos = own_group + jnp.arange(local_rows, dtype=jnp.int32)
    key_pos = jnp.arange(cluster_rows, dtype=jnp.int32)
    attention_mask_matrix = (key_pos[None, :] <= query_pos[:, None]) & (
        query_seg[:, None] == key_seg[None, :]
    )
    rotary_cosine, rotary_sine = rope_tables(query_pos, HEAD_SIZE)
    normed_f, inv_in = rms_forward(tokens, gain_sequence[0])
    normed_in = normed_f.astype(jnp.bfloat16)
    projection_output = jnp.dot(normed_in, collected_rows[0], preferred_element_type=jnp.float32)
    query_raw = projection_output[:, : QUERY_HEADS * HEAD_SIZE].reshape(
        local_rows, QUERY_HEADS, HEAD_SIZE
    )
    key_unrotated = projection_output[
        :, QUERY_HEADS * HEAD_SIZE : (QUERY_HEADS + KEY_VALUE_HEADS) * HEAD_SIZE
    ].reshape(local_rows, KEY_VALUE_HEADS, HEAD_SIZE)
    value_lowprec = projection_output[:, (QUERY_HEADS + KEY_VALUE_HEADS) * HEAD_SIZE :].astype(
        jnp.bfloat16
    )
    query_norm_output, inv_query = rms_forward(query_raw, gain_sequence[1])
    key_norm, key_inverse_norm = rms_forward(key_unrotated, gain_sequence[2])
    query_lowprec = (
        rotary_embed_apply(query_norm_output, rotary_cosine, rotary_sine)
        .astype(jnp.bfloat16)
        .reshape(local_rows, KEY_VALUE_HEADS, cluster_size, HEAD_SIZE)
    )
    key_lowprec = rotary_embed_apply(key_norm, rotary_cosine, rotary_sine).astype(jnp.bfloat16)
    kv_pair = jnp.stack([key_lowprec.reshape(local_rows, key_value_width), value_lowprec])
    key_value_span = lax.all_gather(kv_pair, "fsdp", axis=1, tiled=True)
    span_keys = key_value_span[0].reshape(cluster_rows, KEY_VALUE_HEADS, HEAD_SIZE)
    span_values = key_value_span[1].reshape(cluster_rows, KEY_VALUE_HEADS, HEAD_SIZE)
    attention_lowprec, log_partition_sum = attend_forward(
        query_lowprec, span_keys, span_values, attention_mask_matrix
    )
    attn_flat = attention_lowprec.reshape(local_rows, QUERY_HEADS * HEAD_SIZE)
    mid_stream = tokens + jnp.dot(attn_flat, collected_rows[1], preferred_element_type=jnp.float32)
    normed_g, inv_mid = rms_forward(mid_stream, gain_sequence[3])
    normed_mid = normed_g.astype(jnp.bfloat16)
    gate_up = jnp.dot(normed_mid, collected_rows[2], preferred_element_type=jnp.float32)
    gate_part = gate_up[:, :FF]
    up_part = gate_up[:, FF:]
    sigmoid_gate = jax.nn.sigmoid(gate_part)
    hidden = (gate_part * sigmoid_gate * up_part).astype(jnp.bfloat16)
    output = mid_stream + jnp.dot(hidden, collected_rows[3], preferred_element_type=jnp.float32)
    cot_low = cotangent.astype(jnp.bfloat16)
    grad_down = tdot(hidden, cot_low)
    d_hidden = transposed_product(cot_low, collected_rows[3])
    d_gate = d_hidden * up_part * sigmoid_gate * (1.0 + gate_part * (1.0 - sigmoid_gate))
    d_up = d_hidden * gate_part * sigmoid_gate
    d_gate_up = jnp.concatenate([d_gate, d_up], axis=1).astype(jnp.bfloat16)
    grad_gate_up = tdot(normed_mid, d_gate_up)
    d_normed_mid = transposed_product(d_gate_up, collected_rows[2])
    back_mid, grad_ffn_gain = root_mean_square_reverse(
        mid_stream, inv_mid, gain_sequence[3], d_normed_mid
    )
    d_mid = cotangent + back_mid
    middle_cotangent_lowprec = d_mid.astype(jnp.bfloat16)
    grad_out_proj = tdot(attn_flat, middle_cotangent_lowprec)
    attention_cotangent = (
        transposed_product(middle_cotangent_lowprec, collected_rows[1])
        .astype(jnp.bfloat16)
        .reshape(local_rows, KEY_VALUE_HEADS, cluster_size, HEAD_SIZE)
    )
    query_lowprec_gradient, grad_kwin, grad_vwin = attention_reverse_pass(
        query_lowprec,
        span_keys,
        span_values,
        attention_mask_matrix,
        attention_lowprec,
        log_partition_sum,
        attention_cotangent,
    )
    kv_grads = jnp.stack(
        [
            grad_kwin.reshape(cluster_rows, key_value_width),
            grad_vwin.reshape(cluster_rows, key_value_width),
        ]
    )
    local_key_value = lax.psum_scatter(
        kv_grads.astype(jnp.bfloat16), "fsdp", scatter_dimension=1, tiled=True
    ).astype(jnp.float32)
    d_query, grad_query_gain = root_mean_square_reverse(
        query_raw,
        inv_query,
        gain_sequence[1],
        rotary_embed_invert(
            query_lowprec_gradient.reshape(local_rows, QUERY_HEADS, HEAD_SIZE),
            rotary_cosine,
            rotary_sine,
        ),
    )
    key_cotangent, key_gain_gradient = root_mean_square_reverse(
        key_unrotated,
        key_inverse_norm,
        gain_sequence[2],
        rotary_embed_invert(
            local_key_value[0].reshape(local_rows, KEY_VALUE_HEADS, HEAD_SIZE),
            rotary_cosine,
            rotary_sine,
        ),
    )
    d_projected = jnp.concatenate(
        [
            d_query.reshape(local_rows, -1),
            key_cotangent.reshape(local_rows, -1),
            local_key_value[1],
        ],
        axis=1,
    ).astype(jnp.bfloat16)
    grad_qkv = tdot(normed_in, d_projected)
    d_normed_in = transposed_product(d_projected, collected_rows[0])
    back_in, grad_attn_gain = root_mean_square_reverse(
        tokens, inv_in, gain_sequence[0], d_normed_in
    )
    grad_tokens = d_mid + back_in
    grads_local = (
        grad_qkv,
        grad_out_proj,
        grad_gate_up,
        grad_down,
        grad_attn_gain,
        grad_query_gain,
        key_gain_gradient,
        grad_ffn_gain,
    )
    grad_share = (
        lax.psum_scatter(
            grads_local[0].astype(jnp.bfloat16), "fsdp", scatter_dimension=0, tiled=True
        ).astype(jnp.float32),
        lax.psum_scatter(
            grads_local[1].astype(jnp.bfloat16), "fsdp", scatter_dimension=0, tiled=True
        ).astype(jnp.float32),
        lax.psum_scatter(
            grads_local[2].astype(jnp.bfloat16), "fsdp", scatter_dimension=0, tiled=True
        ).astype(jnp.float32),
        lax.psum_scatter(
            grads_local[3].astype(jnp.bfloat16), "fsdp", scatter_dimension=0, tiled=True
        ).astype(jnp.float32),
        lax.psum_scatter(
            grads_local[4].astype(jnp.bfloat16), "fsdp", scatter_dimension=0, tiled=True
        ).astype(jnp.float32),
        lax.psum_scatter(
            grads_local[5].astype(jnp.bfloat16), "fsdp", scatter_dimension=0, tiled=True
        ).astype(jnp.float32),
        lax.psum_scatter(
            grads_local[6].astype(jnp.bfloat16), "fsdp", scatter_dimension=0, tiled=True
        ).astype(jnp.float32),
        lax.psum_scatter(
            grads_local[7].astype(jnp.bfloat16), "fsdp", scatter_dimension=0, tiled=True
        ).astype(jnp.float32),
    )
    grad_total = (
        lax.psum(grad_share[0].astype(jnp.bfloat16), "rep").astype(jnp.float32),
        lax.psum(grad_share[1].astype(jnp.bfloat16), "rep").astype(jnp.float32),
        lax.psum(grad_share[2].astype(jnp.bfloat16), "rep").astype(jnp.float32),
        lax.psum(grad_share[3].astype(jnp.bfloat16), "rep").astype(jnp.float32),
        lax.psum(grad_share[4].astype(jnp.bfloat16), "rep").astype(jnp.float32),
        lax.psum(grad_share[5].astype(jnp.bfloat16), "rep").astype(jnp.float32),
        lax.psum(grad_share[6].astype(jnp.bfloat16), "rep").astype(jnp.float32),
        lax.psum(grad_share[7].astype(jnp.bfloat16), "rep").astype(jnp.float32),
    )
    return (
        output,
        grad_tokens,
        grad_total[0],
        grad_total[1],
        grad_total[2],
        grad_total[3],
        grad_total[4],
        grad_total[5],
        grad_total[6],
        grad_total[7],
    )


def solution(mesh):
    placed = (
        P(("rep", "fsdp"), None),
        P(),
        P(("rep", "fsdp"), None),
        P("fsdp", None),
        P("fsdp", None),
        P("fsdp", None),
        P("fsdp", None),
        P("fsdp"),
        P("fsdp"),
        P("fsdp"),
        P("fsdp"),
    )
    return jax.shard_map(
        body,
        mesh=mesh,
        in_specs=placed,
        out_specs=(
            P(("rep", "fsdp"), None),
            P(("rep", "fsdp"), None),
            P("fsdp", None),
            P("fsdp", None),
            P("fsdp", None),
            P("fsdp", None),
            P("fsdp"),
            P("fsdp"),
            P("fsdp"),
            P("fsdp"),
        ),
        check_vma=False,
    )
```

profile of v0, /device:TPU:0, one launch (start us, length us, event | category | flops | bytes accessed | tf_op | source)
XLA Modules:
  0.0 968.5 jit_solution(10914518348454304523)
XLA Ops:
  8.0 13.6 %all-gather = bf16[8,1,128]{2,1,0:T(2,128)(2,1)S(1)} all-gather(bf16[1,1,128]{2,1,0:T(2,128)(2,1)} %bitcast.157), channel_id=1, replica_groups=mesh['rep'=4,'fsdp'=8] {'fsdp'}, dimensions={0}, use_global_device_ids=true | all-gather | bytes 2304 | tf_op jit(solution)/shard_map/all_gather | solution.py:144
  25.3 15.0 %all-reduce.7 = (bf16[64]{0:T(256)(128)(2,1)S(1)}, bf16[64]{0:T(256)(128)(2,1)S(1)}) all-reduce(bf16[64]{0:T(256)(128)(2,1)S(1)} %dynamic-update-slice, bf16[64]{0:T(256)(128)(2,1)S(1)} %dynamic-update-slice.1), channel_id=1, replica_groups=mesh['rep'=4,'fsdp'=8] {'fsdp'}, use_global_device_ids=true, to_apply=%add | all-reduce | flops 128 | bytes 512
  42.8 16.7 %all-gather.8.cloned.1.call-done = bf16[1024,2048]{1,0:T(8,128)(2,1)} async-done(((bf16[128,2048]{1,0:T(8,128)(2,1)}), bf16[1024,2048]{1,0:T(8,128)(2,1)}) %all-gather.8.cloned.1.call-update) | async-done | bytes 4194320 | tf_op jit(solution)/shard_map/all_gather | solution.py:140
  59.5 3.1 fusion.40
  68.1 10.1 %all-gather.1 = bf16[8,1,128]{2,1,0:T(2,128)(2,1)S(1)} all-gather(bf16[1,1,128]{2,1,0:T(2,128)(2,1)S(1)} %bitcast.158), channel_id=1, replica_groups=mesh['rep'=4,'fsdp'=8] {'fsdp'}, dimensions={0}, use_global_device_ids=true | all-gather | bytes 2304 | tf_op jit(solution)/shard_map/all_gather | solution.py:147
  79.7 13.1 %all-gather.10.cloned.1.call-done = bf16[2,1024,512]{2,1,0:T(8,128)(2,1)} async-done(((bf16[2,128,512]{2,1,0:T(8,128)(2,1)}), bf16[2,1024,512]{2,1,0:T(8,128)(2,1)}) %all-gather.10.cloned.1.call-update) | async-done | bytes 2097168 | tf_op jit(solution)/shard_map/all_gather | solution.py:179
  92.8 2.6 fusion.42
  99.8 2.0 fusion.3
  103.1 2.5 fusion.13
  105.7 17.3 %all-gather.12.cloned.1.call-done = bf16[1024,1024]{1,0:T(8,128)(2,1)} async-done(((bf16[128,1024]{1,0:T(8,128)(2,1)}), bf16[1024,1024]{1,0:T(8,128)(2,1)}) %all-gather.12.cloned.1.call-update) | async-done | bytes 2097168 | tf_op jit(solution)/shard_map/all_gather | solution.py:141
  123.0 2.1 multiply_reduce_fusion.6
  126.3 165.9 %all-gather.14.cloned.1.call-done = bf16[1024,9216]{1,0:T(8,128)(2,1)} async-done(((bf16[128,9216]{1,0:T(8,128)(2,1)}), bf16[1024,9216]{1,0:T(8,128)(2,1)}) %all-gather.14.cloned.1.call-update) | async-done | bytes 18874384 | tf_op jit(solution)/shard_map/all_gather | solution.py:142
  292.2 11.3 %fusion.41 = f32[128,9216]{1,0:T(8,128)} fusion(bf16[1024,9216]{1,0:T(8,128)(2,1)} %all-gather.14.cloned.1.call-done, f32[128,1024]{1,0:T(8,128)S(1)} %get-tuple-element.62, f32[1024]{0:T(1024)S(1)} %bitcast.143, f32[128]{0:T(128)S(1)} %get-tuple-element.58), kind=kOutput, calls=%fused_computation.114 | convolution fusion | flops 2416312320 | bytes 24121856 | tf_op jit(solution)/shard_map/dot_general | solution.py:189
  303.5 79.1 %all-gather.16.cloned.1.call-done = bf16[4608,1024]{1,0:T(8,128)(2,1)} async-done(((bf16[576,1024]{1,0:T(8,128)(2,1)}), bf16[4608,1024]{1,0:T(8,128)(2,1)}) %all-gather.16.cloned.1.call-update) | async-done | bytes 9437200 | tf_op jit(solution)/shard_map/all_gather | solution.py:143
  382.6 8.9 multiply_convert_fusion.1
  391.6 12.6 %multiply_reduce_fusion = (bf16[1024]{0:T(1024)(128)(2,1)}, f32[128]{0:T(128)S(1)}, f32[128,1024]{1,0:T(8,128)S(1)}) fusion(f32[128,1024]{1,0:T(8,128)S(1)} %get-tuple-element.62, f32[128]{0:T(128)S(1)} %copy-done.47, f32[1024]{0:T(1024)S(1)} %bitcast.144, bf16[1024,9216]{1,0:T(8,128)(2,1)} %all-gather.14.cloned.1.call-done, ...), kind=kOutput, calls=%fused_computation.39 | convolution fusion | flops 2421423104 | bytes 22289408 | tf_op jit(solution)/shard_map/dot_general | solution.py:121
  406.7 1.8 copy.100
  409.7 6.5 bitcast_convert_fusion
  416.3 5.7 fusion.2
  422.0 2.0 copy-done.1
  424.0 2.4 bitcast_convert_fusion.1
  426.4 2.3 copy.108
  428.7 2.3 copy.109
  431.0 3.1 pad_maximum_fusion.1
  434.1 3.1 convolution_convert_fusion.3
  443.5 2.0 copy.103
  447.0 2.1 copy.104
  450.5 1.8 copy.112
  453.7 1.8 copy.113
  455.5 3.1 fusion.44
  460.5 2.0 copy.105
  462.5 2.0 copy.102
  464.6 2.5 subtract_convert_fusion
  470.4 1.8 copy.110
  478.4 4.4 convolution_convert_fusion.2
  483.8 5.1 convolution_convert_fusion.1
  489.6 10.9 %convolution_convert_fusion = bf16[1024,9216]{1,0:T(8,128)(2,1)} fusion(bf16[128,4608]{1,0:T(8,128)(2,1)} %copy-done.27, bf16[128,4608]{1,0:T(8,128)(2,1)} %copy-done.26, f32[128,1024]{1,0:T(8,128)S(1)} %get-tuple-element.62, f32[1024]{0:T(1024)S(1)} %bitcast.146, f32[128]{0:T(128)S(1)} %copy-done.48), kind=kOutput, calls=%fused_computation | convolution fusion | flops 2430468096 | bytes 21762560 | tf_op jit(solution)/shard_map/dot_general | solution.py:115
  500.8 4.7 reduce-scatter.10.cloned.1.call-done
  505.5 51.2 %reduce-scatter.8.cloned.1.call-done = bf16[128,2048]{1,0:T(8,128)(2,1)} async-done(((bf16[1024,2048]{1,0:T(8,128)(2,1)}), bf16[128,2048]{1,0:T(8,128)(2,1)}) %reduce-scatter.8.cloned.1.call-update) | async-done | bytes 524304 | tf_op jit(solution)/shard_map/reduce_scatter | solution.py:277
  556.7 100.2 %reduce-scatter.14.cloned.1.call-done = bf16[576,1024]{1,0:T(8,128)(2,1)} async-done(((bf16[4608,1024]{1,0:T(8,128)(2,1)}), bf16[576,1024]{1,0:T(8,128)(2,1)}) %reduce-scatter.14.cloned.1.call-update) | async-done | bytes 1179664 | tf_op jit(solution)/shard_map/reduce_scatter | solution.py:286
  657.0 188.6 %reduce-scatter.12.cloned.1.call-done = bf16[128,9216]{1,0:T(8,128)(2,1)} async-done(((bf16[1024,9216]{1,0:T(8,128)(2,1)}), bf16[128,9216]{1,0:T(8,128)(2,1)}) %reduce-scatter.12.cloned.1.call-update) | async-done | bytes 2359312 | tf_op jit(solution)/shard_map/reduce_scatter | solution.py:283
  852.3 3.3 fusion.15
  855.5 5.9 convolution_add_fusion.1
  863.5 4.0 multiply_reduce_fusion.1
  867.5 14.3 %all-reduce.6 = (bf16[1024]{0:T(1024)(128)(2,1)S(1)}, bf16[64]{0:T(256)(128)(2,1)S(1)}, bf16[64]{0:T(256)(128)(2,1)S(1)}, bf16[1024]{0:T(1024)(128)(2,1)S(1)}) all-reduce(bf16[1024]{0:T(1024)(128)(2,1)S(1)} %get-tuple-element.12, bf16[64]{0:T(256)(128)(2,1)S(1)} %copy-done.56, ...), channel_id=7, replica_groups=mesh['rep'=4,'fsdp'=8] {'fsdp'}, use_global_device_ids=true, to_apply=%region_21.22.clone | all-reduce | flops 2176 | bytes 8704
  882.0 10.3 %all-reduce.8 = (bf16[128]{0:T(256)(128)(2,1)S(1)}, bf16[8]{0:T(256)(128)(2,1)S(1)}, bf16[8]{0:T(256)(128)(2,1)S(1)}, bf16[128]{0:T(256)(128)(2,1)S(1)}) all-reduce(bf16[128]{0:T(256)(128)(2,1)S(1)} %dynamic-slice.3, bf16[8]{0:T(256)(128)(2,1)S(1)} %dynamic-slice.5, ...), channel_id=1, replica_groups=mesh['rep'=4,'fsdp'=8] {'rep'}, use_global_device_ids=true, to_apply=%region_22.23 | all-reduce | flops 272 | bytes 1088 | tf_op jit(solution)/shard_map/psum | solution.py:307
  895.4 58.3 %all-reduce.12.cloned.1.call-done = (bf16[128,2048]{1,0:T(8,128)(2,1)}, bf16[128,1024]{1,0:T(8,128)(2,1)}, bf16[128,9216]{1,0:T(8,128)(2,1)}, bf16[576,1024]{1,0:T(8,128)(2,1)}) async-done(((bf16[128,2048]{1,0:T(8,128)(2,1)}, bf16[128,1024]{1,0:T(8,128)(2,1)}, bf16[128,9216]{1,0:T(8,128)(2,1)}, bf16[576,1024]{1,0:T(8,128)(2,1)}), (bf16[128,2048]{1,0:T(8,128)(2,1)}, bf16[128,1024]{1,0:T(8,128)(2,1)}, ...) | async-done | bytes 4325392 | tf_op jit(solution)/shard_map/psum | solution.py:303
  953.7 4.4 convert_element_type.164
  (233 shorter events, 61.6 us)
Async XLA Ops:
  7.2 52.3 %all-gather.8.cloned.1.call-start = ((), (), s32[]{:S(2)}) async-start(), calls=%async_computation.5 | async-start | bytes 4718592 | tf_op jit(solution)/shard_map/all_gather | solution.py:140
  7.9 84.9 %all-gather.10.cloned.1.call-start = ((), (), s32[]{:S(2)}) async-start(), calls=%async_computation.6 | async-start | bytes 2359296 | tf_op jit(solution)/shard_map/all_gather | solution.py:179
  40.3 26.4 %copy-start.61 = (bf16[64]{0:T(256)(128)(2,1)}, bf16[64]{0:T(256)(128)(2,1)S(1)}, u32[]{:S(2)}) copy-start(bf16[64]{0:T(256)(128)(2,1)S(1)} %get-tuple-element.19) | copy-start | bytes 388
  40.3 23.4 %copy-start.55 = (f32[64]{0:T(128)}, f32[64]{0:T(128)S(1)}, u32[]{:S(2)}) copy-start(f32[64]{0:T(128)S(1)} %convert_element_type.142) | copy-start | bytes 772
  42.6 20.1 %copy-start.50 = (f32[128]{0:T(128)}, f32[128]{0:T(128)S(1)}, u32[]{:S(2)}) copy-start(f32[128]{0:T(128)S(1)} %get-tuple-element.56) | copy-start | bytes 1540
  42.8 36.8 %copy-start.39 = (f32[128,32]{0,1:T(8,128)}, f32[128,32]{0,1:T(8,128)S(1)}, u32[]{:S(2)}) copy-start(f32[128,32]{0,1:T(8,128)S(1)} %get-tuple-element.51) | copy-start | bytes 49156
  42.8 36.8 %copy-start.41 = (f32[128,32]{0,1:T(8,128)}, f32[128,32]{0,1:T(8,128)S(1)}, u32[]{:S(2)}) copy-start(f32[128,32]{0,1:T(8,128)S(1)} %get-tuple-element.52) | copy-start | bytes 49156
  62.6 15.8 %copy-start.8 = (f32[128,2048]{1,0:T(8,128)}, f32[128,2048]{1,0:T(8,128)S(1)}, u32[]{:S(2)}) copy-start(f32[128,2048]{1,0:T(8,128)S(1)} %fusion.40) | copy-start | bytes 3145732
  62.7 15.5 %copy-start.12 = (f32[128,512]{1,0:T(8,128)}, f32[128,512]{1,0:T(8,128)S(1)}, u32[]{:S(2)}) copy-start(f32[128,512]{1,0:T(8,128)S(1)} %slice.71) | copy-start | bytes 786436
  64.7 58.3 %all-gather.12.cloned.1.call-start = ((), (), s32[]{:S(2)}) async-start(), calls=%async_computation.7 | async-start | bytes 2359296 | tf_op jit(solution)/shard_map/all_gather | solution.py:141
  65.4 226.8 %all-gather.14.cloned.1.call-start = ((), (), s32[]{:S(2)}) async-start(), calls=%async_computation.8 | async-start | bytes 21233664 | tf_op jit(solution)/shard_map/all_gather | solution.py:142
  66.0 316.6 %all-gather.16.cloned.1.call-start = ((), (), s32[]{:S(2)}) async-start(), calls=%async_computation.9 | async-start | bytes 10616832 | tf_op jit(solution)/shard_map/all_gather | solution.py:143
  66.6 402.0 %reduce-scatter.6.cloned.1.call-start = ((), (), s32[]{:S(2)}) async-start(), calls=%async_computation.10 | async-start | bytes 2359296 | tf_op jit(solution)/shard_map/reduce_scatter | solution.py:229
  66.7 28.8 %copy-start.52 = (f32[64]{0:T(128)}, f32[64]{0:T(128)S(1)}, u32[]{:S(2)}) copy-start(f32[64]{0:T(128)S(1)} %convert_element_type.145) | copy-start | bytes 772
  78.4 23.3 %copy-start.20 = (pred[128,1024]{0,1:T(8,128)(4,1)}, pred[128,1024]{0,1:T(8,128)(4,1)S(1)}, u32[]{:S(2)}) copy-start(pred[128,1024]{0,1:T(8,128)(4,1)S(1)} %fusion.18) | copy-start | bytes 393220
  78.5 17.0 %copy-start.10 = (f32[128,1024]{1,0:T(8,128)}, f32[128,1024]{1,0:T(8,128)S(1)}, u32[]{:S(2)}) copy-start(f32[128,1024]{1,0:T(8,128)S(1)} %slice.77) | copy-start | bytes 1572868
  78.7 18.3 %copy-start.4 = (f32[128,1024]{0,1:T(8,128)}, f32[128,1024]{0,1:T(8,128)S(1)}, u32[]{:S(2)}) copy-start(f32[128,1024]{0,1:T(8,128)S(1)} %copy.98) | copy-start | bytes 1572868
  79.7 18.6 %copy-start.22 = (bf16[128,16,32]{0,2,1:T(8,128)(2,1)}, bf16[128,16,32]{0,2,1:T(8,128)(2,1)S(1)}, u32[]{:S(2)}) copy-start(bf16[128,16,32]{0,2,1:T(8,128)(2,1)S(1)} %get-tuple-element.35) | copy-start | bytes 393220
  79.7 18.6 %copy-start.24 = (bf16[128,16,32]{0,2,1:T(8,128)(2,1)}, bf16[128,16,32]{0,2,1:T(8,128)(2,1)S(1)}, u32[]{:S(2)}) copy-start(bf16[128,16,32]{0,2,1:T(8,128)(2,1)S(1)} %get-tuple-element.36) | copy-start | bytes 393220
  103.1 19.9 %copy-start.2 = (f32[128,1024]{1,0:T(8,128)S(1)}, f32[128,1024]{1,0:T(8,128)}, u32[]{:S(2)}) copy-start(f32[128,1024]{1,0:T(8,128)} %param.11) | copy-start | bytes 1572868
  105.7 197.9 %copy-start.17 = (bf16[8,64,2,128]{3,1,2,0:T(8,128)(2,1)}, bf16[8,64,2,128]{3,1,2,0:T(8,128)(2,1)S(1)}, u32[]{:S(2)}) copy-start(bf16[8,64,2,128]{3,1,2,0:T(8,128)(2,1)S(1)} %fusion.13) | copy-start | bytes 786436
  125.7 177.8 %copy-start.46 = (f32[128]{0:T(128)}, f32[128]{0:T(128)S(1)}, u32[]{:S(2)}) copy-start(f32[128]{0:T(128)S(1)} %get-tuple-element.58) | copy-start | bytes 1540
  382.6 8.9 copy-start.47
  391.5 12.7 %copy-start.26 = (bf16[128,4608]{1,0:T(8,128)(2,1)}, bf16[128,4608]{1,0:T(8,128)(2,1)S(1)}, u32[]{:S(2)}) copy-start(bf16[128,4608]{1,0:T(8,128)(2,1)S(1)} %get-tuple-element.28) | copy-start | bytes 3538948
  391.6 12.7 %copy-start.27 = (bf16[128,4608]{1,0:T(8,128)(2,1)}, bf16[128,4608]{1,0:T(8,128)(2,1)S(1)}, u32[]{:S(2)}) copy-start(bf16[128,4608]{1,0:T(8,128)(2,1)S(1)} %get-tuple-element.29) | copy-start | bytes 3538948
  391.6 12.6 %copy-start.18 = (f32[128,1024]{1,0:T(8,128)S(1)}, f32[128,1024]{1,0:T(8,128)}, u32[]{:S(2)}) copy-start(f32[128,1024]{1,0:T(8,128)} %param.13) | copy-start | bytes 1572868
  391.6 12.6 %copy-start.58 = (f32[128]{0:T(128)S(1)}, f32[128]{0:T(128)}, u32[]{:S(2)}) copy-start(f32[128]{0:T(128)} %get-tuple-element.57) | copy-start | bytes 1540
  391.6 13.6 %copy-start.3 = (bf16[1024,1024]{1,0:T(8,128)(2,1)S(1)}, bf16[1024,1024]{1,0:T(8,128)(2,1)}, u32[]{:S(2)}) copy-start(bf16[1024,1024]{1,0:T(8,128)(2,1)} %all-gather.12.cloned.1.call-done) | copy-start | bytes 6291460
  409.7 6.6 copy-start.21
  409.7 6.6 copy-start.34
  409.7 6.5 copy-start.35
  409.7 6.5 copy-start.49
  416.2 7.8 copy-start.23
  416.3 7.8 copy-start.25
  434.0 71.5 %reduce-scatter.10.cloned.1.call-start = ((), (), s32[]{:S(2)}) async-start(), calls=%async_computation.12 | async-start | bytes 2359296 | tf_op jit(solution)/shard_map/reduce_scatter | solution.py:280
  437.2 119.5 %reduce-scatter.8.cloned.1.call-start = ((), (), s32[]{:S(2)}) async-start(), calls=%async_computation.11 | async-start | bytes 4718592 | tf_op jit(solution)/shard_map/reduce_scatter | solution.py:277
  482.8 174.2 %reduce-scatter.14.cloned.1.call-start = ((), (), s32[]{:S(2)}) async-start(), calls=%async_computation.14 | async-start | bytes 10616832 | tf_op jit(solution)/shard_map/reduce_scatter | solution.py:286
  488.9 356.6 %reduce-scatter.12.cloned.1.call-start = ((), (), s32[]{:S(2)}) async-start(), calls=%async_computation.13 | async-start | bytes 21233664 | tf_op jit(solution)/shard_map/reduce_scatter | solution.py:283
  500.5 346.5 %copy-start.11 = (f32[128,1024]{1,0:T(8,128)S(1)}, f32[128,1024]{1,0:T(8,128)}, u32[]{:S(2)}) copy-start(f32[128,1024]{1,0:T(8,128)} %copy-done.10) | copy-start | bytes 1572868
  500.5 347.7 %copy-start.45 = (f32[128,8]{0,1:T(8,128)S(1)}, f32[128,8]{0,1:T(8,128)}, u32[]{:S(2)}) copy-start(f32[128,8]{0,1:T(8,128)} %copy-done.44) | copy-start | bytes 12292
  500.5 347.8 %copy-start.13 = (f32[128,512]{1,0:T(8,128)S(1)}, f32[128,512]{1,0:T(8,128)}, u32[]{:S(2)}) copy-start(f32[128,512]{1,0:T(8,128)} %copy-done.12) | copy-start | bytes 786436
  500.5 350.4 %copy-start.15 = (f32[128,16,32]{0,2,1:T(8,128)S(1)}, f32[128,16,32]{0,2,1:T(8,128)}, u32[]{:S(2)}) copy-start(f32[128,16,32]{0,2,1:T(8,128)} %copy-done.14) | copy-start | bytes 786436
  500.6 453.1 %all-reduce.12.cloned.1.call-start = ((), (), s32[]{:S(2)}) async-start(), calls=%async_computation.15 | async-start | bytes 8650752 | tf_op jit(solution)/shard_map/psum | solution.py:303
  855.5 6.2 copy-start.30
  855.5 7.9 copy-start.36
  855.5 7.9 copy-start.51
  861.7 32.7 %copy-start.7 = (f32[128,1024]{1,0:T(8,128)S(1)}, f32[128,1024]{1,0:T(8,128)}, u32[]{:S(2)}) copy-start(f32[128,1024]{1,0:T(8,128)} %copy-done.6) | copy-start | bytes 1572868
  861.7 32.7 %copy-start.57 = (f32[128]{0:T(128)S(1)}, f32[128]{0:T(128)}, u32[]{:S(2)}) copy-start(f32[128]{0:T(128)} %get-tuple-element.55) | copy-start | bytes 1540
  (25 other events, 76.5 us)
Sparse Core Ops, SparseCore 0:
  9.6 49.8 all-gather.7
  64.8 27.9 all-gather.9
  94.4 28.5 all-gather.11
  124.5 167.6 all-gather.13
  293.7 88.8 all-gather.15
  434.1 34.4 reduce-scatter.5
  470.9 34.5 reduce-scatter.9
  508.4 48.2 reduce-scatter.7
  559.0 97.8 reduce-scatter.13
  659.2 186.3 reduce-scatter.11
  849.3 104.2 all-reduce.11
where the time goes:
time: 972 us; the launch traced here: 968 us
  waiting for transfers between devices  699 us (72%)
  matrix products  94.7 us (10%)
  blocking collectives  63.3 us (7%)
  local copies, waits for them, and re-layouts  56.8 us (6%)
  other arithmetic  36.6 us (4%)
  between operations  16.9 us (2%)
    reduce_scatter x1, waiting for transfers between devices, body(): lax.psum_scatter(grads_local[2].astype(jnp.bfloat16), 'fsdp', scatter_dim...  189 us
    all_gather x1, waiting for transfers between devices, body(): lax.all_gather(shards[2], 'fsdp', axis=0, tiled=True)  166 us
    reduce_scatter x1, waiting for transfers between devices, body(): lax.psum_scatter(grads_local[3].astype(jnp.bfloat16), 'fsdp', scatter_dim...  100 us
    all_gather x1, waiting for transfers between devices, body(): lax.all_gather(shards[3], 'fsdp', axis=0, tiled=True)  79.1 us
    psum x1, waiting for transfers between devices, body(): lax.psum(grad_share[0].astype(jnp.bfloat16), 'rep').astype(jnp.float32)  58.3 us
    reduce_scatter x1, waiting for transfers between devices, body(): lax.psum_scatter(grads_local[0].astype(jnp.bfloat16), 'fsdp', scatter_dim...  51.2 us
    unnamed x2, blocking collectives  29.3 us
    dot_general x4, matrix products, transposed_product(): lax.dot_general(left_arr, right_arr, (((1,), (1,)), ((), ())), preferred_...  27 us
  transfers between devices with their start and end apart: 11, of which 11 were waited for; matrix products, arithmetic and copies ran while one was open for 12% of the time, Pallas kernels for 0%

commit v1 on v0

--- a/solution.py
+++ b/solution.py
@@ -126,6 +126,28 @@
 def body(
     tokens, segment_ids, cotangent, w_qkv, w_out, w_gate_up, w_down, g_attn, g_query, g_key, g_ffn
 ):
+
+    def indices_plan(sheet, device_axis):
+        mat_out = lax.axis_size(device_axis)
+        part_next = lax.axis_index(device_axis)
+        now, inter, step_out = (mat_out, part_next, sheet.shape[0])
+        piece_next, e_next = (sheet, 1)
+        while e_next < now:
+            piece_next = jnp.concatenate(
+                [
+                    piece_next,
+                    lax.ppermute(
+                        piece_next,
+                        axis_name=device_axis,
+                        perm=[(t, (t - e_next) % now) for t in range(now)],
+                    ),
+                ],
+                0,
+            )
+            e_next = 2 * e_next
+        v_now = jnp.roll(piece_next, inter * step_out, 0)
+        return v_now
+
     local_rows = tokens.shape[0]
     cluster_size = QUERY_HEADS // KEY_VALUE_HEADS
     seq_devices = lax.axis_size("fsdp")
@@ -140,7 +162,7 @@
         lax.all_gather(shards[0], "fsdp", axis=0, tiled=True),
         lax.all_gather(shards[1], "fsdp", axis=0, tiled=True),
         lax.all_gather(shards[2], "fsdp", axis=0, tiled=True),
-        lax.all_gather(shards[3], "fsdp", axis=0, tiled=True),
+        indices_plan(shards[3], "fsdp"),
         lax.all_gather(shards[4], "fsdp", axis=0, tiled=True),
         lax.all_gather(shards[5], "fsdp", axis=0, tiled=True),
         lax.all_gather(shards[6], "fsdp", axis=0, tiled=True),

time: 972 us -> 1170 us (1.20)
  blocking collectives: 63.3 us -> 243 us
    ppermute x0 -> x3, waiting for transfers between devices: none -> 254 us  [indices_plan(): lax.ppermute(piece_next, axis_name=device_axis, perm=[(t, (t - e_next) %...]
    all_gather x1, blocking collectives: 10.1 us -> 189 us  [body(): lax.all_gather(shards[7], 'fsdp', axis=0, tiled=True)]
    all_gather x1, waiting for transfers between devices: 166 us -> 0.01 us  [body(): lax.all_gather(shards[2], 'fsdp', axis=0, tiled=True)]
    all_gather x1 -> x0, waiting for transfers between devices: 79.1 us -> none  [body(): lax.all_gather(shards[3], 'fsdp', axis=0, tiled=True)]
    reduce_scatter x1, waiting for transfers between devices: 1.6 us -> 33.2 us  [body(): lax.psum_scatter(kv_grads.astype(jnp.bfloat16), 'fsdp', scatter_dimension...]
    all_gather x1, waiting for transfers between devices: 17.3 us -> 0.02 us  [body(): lax.all_gather(shards[1], 'fsdp', axis=0, tiled=True)]
    all_gather x1, waiting for transfers between devices: 13.1 us -> 0.01 us  [body(): key_value_span = lax.all_gather(kv_pair, 'fsdp', axis=1, tiled=True)]
    unnamed x133 -> x128, local copies, waits for them, and re-layouts: 10.5 us -> 23.3 us
  transfers between devices with their start and end apart: 11 -> 13, of which waited for: 11 -> 10; matrix products, arithmetic and copies ran while one was open for 12% -> 11% of each run, Pallas kernels for 0% -> 0%
where the time goes in v1:
time: 1170 us
  waiting for transfers between devices  710 us (61%)
  blocking collectives  243 us (21%)
  matrix products  93.5 us (8%)
  local copies, waits for them, and re-layouts  62.6 us (5%)
  other arithmetic  40.2 us (3%)
  between operations  17.1 us (1%)
    ppermute x3, waiting for transfers between devices, indices_plan(): lax.ppermute(piece_next, axis_name=device_axis, perm=[(t, (t - e_next) %...  254 us
    all_gather x1, blocking collectives, body(): lax.all_gather(shards[7], 'fsdp', axis=0, tiled=True)  189 us
    reduce_scatter x1, waiting for transfers between devices, body(): lax.psum_scatter(grads_local[2].astype(jnp.bfloat16), 'fsdp', scatter_dim...  189 us
    reduce_scatter x1, waiting for transfers between devices, body(): lax.psum_scatter(grads_local[3].astype(jnp.bfloat16), 'fsdp', scatter_dim...  100 us
    psum x1, waiting for transfers between devices, body(): lax.psum(grad_share[0].astype(jnp.bfloat16), 'rep').astype(jnp.float32)  58.6 us
    reduce_scatter x1, waiting for transfers between devices, body(): lax.psum_scatter(grads_local[0].astype(jnp.bfloat16), 'fsdp', scatter_dim...  51.4 us
    reduce_scatter x1, waiting for transfers between devices, body(): lax.psum_scatter(kv_grads.astype(jnp.bfloat16), 'fsdp', scatter_dimension...  33.2 us
    unnamed x2, blocking collectives  29.6 us
  transfers between devices with their start and end apart: 13, of which 10 were waited for; matrix products, arithmetic and copies ran while one was open for 11% of the time, Pallas kernels for 0%

profile of v1, /device:TPU:0, one launch (start us, length us, event | category | flops | bytes accessed | tf_op | source)
XLA Modules:
  0.0 1167.5 jit_solution(2503324477717165499)
XLA Ops:
  8.0 13.6 %all-gather = bf16[8,1,128]{2,1,0:T(2,128)(2,1)S(1)} all-gather(bf16[1,1,128]{2,1,0:T(2,128)(2,1)} %bitcast.157), channel_id=1, replica_groups=mesh['rep'=4,'fsdp'=8] {'fsdp'}, dimensions={0}, use_global_device_ids=true | all-gather | bytes 2304 | tf_op jit(solution)/shard_map/all_gather | solution.py:166
  25.3 15.0 %all-reduce.7 = (bf16[64]{0:T(256)(128)(2,1)S(1)}, bf16[64]{0:T(256)(128)(2,1)S(1)}) all-reduce(bf16[64]{0:T(256)(128)(2,1)S(1)} %dynamic-update-slice, bf16[64]{0:T(256)(128)(2,1)S(1)} %dynamic-update-slice.1), channel_id=1, replica_groups=mesh['rep'=4,'fsdp'=8] {'fsdp'}, use_global_device_ids=true, to_apply=%add | all-reduce | flops 128 | bytes 512
  42.3 17.3 %all-gather.7.cloned.1.call-done = bf16[1024,2048]{1,0:T(8,128)(2,1)} async-done(((bf16[128,2048]{1,0:T(8,128)(2,1)}), bf16[1024,2048]{1,0:T(8,128)(2,1)}) %all-gather.7.cloned.1.call-update) | async-done | bytes 4194320 | tf_op jit(solution)/shard_map/all_gather | solution.py:162
  59.5 3.2 fusion.51
  68.7 30.6 %collective-permute-done = bf16[576,1024]{1,0:T(8,128)(2,1)S(1)} collective-permute-done((bf16[576,1024]{1,0:T(8,128)(2,1)S(1)}, bf16[576,1024]{1,0:T(8,128)(2,1)S(1)}, u32[]{:S(2)}, u32[]{:S(2)}) %collective-permute-start) | collective-permute-done | bytes 1179680 | tf_op jit(solution)/shard_map/ppermute | solution.py:139
  99.5 71.0 %collective-permute-done.1 = bf16[1152,1024]{1,0:T(8,128)(2,1)S(1)} collective-permute-done((bf16[1152,1024]{1,0:T(8,128)(2,1)S(1)}, bf16[1152,1024]{1,0:T(8,128)(2,1)S(1)}, u32[]{:S(2)}, u32[]{:S(2)}) %collective-permute-start.1) | collective-permute-done | bytes 2359328 | tf_op jit(solution)/shard_map/ppermute | solution.py:139
  170.5 2.5 pad_maximum_fusion
  174.9 188.8 %all-gather.1 = bf16[8,1,128]{2,1,0:T(2,128)(2,1)S(1)} all-gather(bf16[1,1,128]{2,1,0:T(2,128)(2,1)S(1)} %bitcast.158), channel_id=1, replica_groups=mesh['rep'=4,'fsdp'=8] {'fsdp'}, dimensions={0}, use_global_device_ids=true | all-gather | bytes 2304 | tf_op jit(solution)/shard_map/all_gather | solution.py:169
  365.7 2.4 constant_dynamic-update-slice_fusion.6
  370.6 2.0 copy.101
  377.0 152.8 %collective-permute-done.2 = bf16[2304,1024]{1,0:T(8,128)(2,1)} collective-permute-done((bf16[2304,1024]{1,0:T(8,128)(2,1)}, bf16[2304,1024]{1,0:T(8,128)(2,1)}, u32[]{:S(2)}, u32[]{:S(2)}) %collective-permute-start.2) | collective-permute-done | bytes 4718624 | tf_op jit(solution)/shard_map/ppermute | solution.py:139
  529.9 5.1 constant_dynamic-update-slice_fusion.4
  538.8 5.0 constant_dynamic-update-slice_fusion
  543.8 2.7 fusion.53
  546.5 1.9 copy.100
  551.3 2.0 fusion.7
  554.5 2.5 fusion.23
  557.0 2.1 multiply_reduce_fusion.6
  559.8 7.9 fusion.52
  567.7 8.9 multiply_convert_fusion.1
  576.7 12.1 %multiply_reduce_fusion = (bf16[1024]{0:T(1024)(128)(2,1)}, f32[128]{0:T(128)S(1)}, f32[128,1024]{1,0:T(8,128)S(1)}) fusion(f32[128,1024]{1,0:T(8,128)S(1)} %get-tuple-element.62, f32[128]{0:T(128)S(1)} %get-tuple-element.58, f32[1024]{0:T(1024)S(1)} %bitcast.144, bf16[1024,9216]{1,0:T(8,128)(2,1)} %all-gather.13.cloned.1.call-done, ...), kind=kOutput, calls=%fused_computation.46 | convolution fusion | flops 2421423104 | bytes 22289408 | tf_op jit(solution)/shard_map/dot_general | solution.py:121
  591.8 6.5 bitcast_convert_fusion
  598.3 5.7 fusion.2
  604.0 2.0 copy-done.1
  606.0 2.4 bitcast_convert_fusion.1
  608.4 2.3 copy.112
  610.7 2.3 copy.113
  613.0 3.1 pad_maximum_fusion.3
  616.1 2.1 convolution_convert_fusion.3
  622.8 3.0 fusion.55
  627.7 2.0 copy.109
  629.7 2.0 copy.106
  631.8 2.5 subtract_convert_fusion
  634.2 33.2 %reduce-scatter.6.cloned.1.call-done = bf16[2,128,512]{2,1,0:T(8,128)(2,1)} async-done(((bf16[2,1024,512]{2,1,0:T(8,128)(2,1)}), bf16[2,128,512]{2,1,0:T(8,128)(2,1)}) %reduce-scatter.6.cloned.1.call-update) | async-done | bytes 262160 | tf_op jit(solution)/shard_map/reduce_scatter | solution.py:251
  677.2 4.4 convolution_convert_fusion.2
  681.8 6.6 convolution_convert_fusion.1
  689.0 10.9 convolution_convert_fusion
  700.0 4.0 reduce-scatter.10.cloned.1.call-done
  704.0 51.4 %reduce-scatter.8.cloned.1.call-done = bf16[128,2048]{1,0:T(8,128)(2,1)} async-done(((bf16[1024,2048]{1,0:T(8,128)(2,1)}), bf16[128,2048]{1,0:T(8,128)(2,1)}) %reduce-scatter.8.cloned.1.call-update) | async-done | bytes 524304 | tf_op jit(solution)/shard_map/reduce_scatter | solution.py:299
  755.5 100.2 %reduce-scatter.14.cloned.1.call-done = bf16[576,1024]{1,0:T(8,128)(2,1)} async-done(((bf16[4608,1024]{1,0:T(8,128)(2,1)}), bf16[576,1024]{1,0:T(8,128)(2,1)}) %reduce-scatter.14.cloned.1.call-update) | async-done | bytes 1179664 | tf_op jit(solution)/shard_map/reduce_scatter | solution.py:308
  855.7 188.8 %reduce-scatter.12.cloned.1.call-done = bf16[128,9216]{1,0:T(8,128)(2,1)} async-done(((bf16[1024,9216]{1,0:T(8,128)(2,1)}), bf16[128,9216]{1,0:T(8,128)(2,1)}) %reduce-scatter.12.cloned.1.call-update) | async-done | bytes 2359312 | tf_op jit(solution)/shard_map/reduce_scatter | solution.py:305
  1050.2 2.2 fusion.25
  1052.4 7.9 fusion.20
  1061.2 4.1 multiply_reduce_fusion.1
  1065.3 14.6 %all-reduce.6 = (bf16[1024]{0:T(1024)(128)(2,1)S(1)}, bf16[64]{0:T(256)(128)(2,1)S(1)}, bf16[64]{0:T(256)(128)(2,1)S(1)}, bf16[1024]{0:T(1024)(128)(2,1)S(1)}) all-reduce(bf16[1024]{0:T(1024)(128)(2,1)S(1)} %get-tuple-element.12, bf16[64]{0:T(256)(128)(2,1)S(1)} %fusion.25, ...), channel_id=7, replica_groups=mesh['rep'=4,'fsdp'=8] {'fsdp'}, use_global_device_ids=true, to_apply=%region_21.22.clone | all-reduce | flops 2176 | bytes 8704
  1080.2 10.5 all-reduce.8
  1093.8 58.6 %all-reduce.12.cloned.1.call-done = (bf16[128,2048]{1,0:T(8,128)(2,1)}, bf16[128,1024]{1,0:T(8,128)(2,1)}, bf16[128,9216]{1,0:T(8,128)(2,1)}, bf16[576,1024]{1,0:T(8,128)(2,1)}) async-done(((bf16[128,2048]{1,0:T(8,128)(2,1)}, bf16[128,1024]{1,0:T(8,128)(2,1)}, bf16[128,9216]{1,0:T(8,128)(2,1)}, bf16[576,1024]{1,0:T(8,128)(2,1)}), (bf16[128,2048]{1,0:T(8,128)(2,1)}, bf16[128,1024]{1,0:T(8,128)(2,1)}, ...) | async-done | bytes 4325392 | tf_op jit(solution)/shard_map/psum | solution.py:325
  1152.4 4.5 convert_element_type.164
  (234 shorter events, 63.1 us)
Async XLA Ops:
  7.2 52.3 %all-gather.7.cloned.1.call-start = ((), (), s32[]{:S(2)}) async-start(), calls=%async_computation.5 | async-start | bytes 4718592 | tf_op jit(solution)/shard_map/all_gather | solution.py:162
  7.9 535.9 %all-gather.9.cloned.1.call-start = ((), (), s32[]{:S(2)}) async-start(), calls=%async_computation.6 | async-start | bytes 2359296 | tf_op jit(solution)/shard_map/all_gather | solution.py:201
  40.3 19.2 %copy-start.52 = (bf16[64]{0:T(256)(128)(2,1)}, bf16[64]{0:T(256)(128)(2,1)S(1)}, u32[]{:S(2)}) copy-start(bf16[64]{0:T(256)(128)(2,1)S(1)} %get-tuple-element.18) | copy-start | bytes 388
  40.3 132.6 %copy-start.54 = (bf16[64]{0:T(256)(128)(2,1)}, bf16[64]{0:T(256)(128)(2,1)S(1)}, u32[]{:S(2)}) copy-start(bf16[64]{0:T(256)(128)(2,1)S(1)} %get-tuple-element.19) | copy-start | bytes 388
  40.3 24.4 %copy-start.49 = (f32[64]{0:T(128)}, f32[64]{0:T(128)S(1)}, u32[]{:S(2)}) copy-start(f32[64]{0:T(128)S(1)} %convert_element_type.142) | copy-start | bytes 772
  42.1 20.7 %copy-start.45 = (f32[128]{0:T(128)}, f32[128]{0:T(128)S(1)}, u32[]{:S(2)}) copy-start(f32[128]{0:T(128)S(1)} %get-tuple-element.56) | copy-start | bytes 1540
  42.2 22.5 %copy-start.32 = (f32[128,32]{0,1:T(8,128)}, f32[128,32]{0,1:T(8,128)S(1)}, u32[]{:S(2)}) copy-start(f32[128,32]{0,1:T(8,128)S(1)} %get-tuple-element.51) | copy-start | bytes 49156
  42.2 22.5 %copy-start.34 = (f32[128,32]{0,1:T(8,128)}, f32[128,32]{0,1:T(8,128)S(1)}, u32[]{:S(2)}) copy-start(f32[128,32]{0,1:T(8,128)S(1)} %get-tuple-element.52) | copy-start | bytes 49156
  59.5 7.9 copy-start.2
  63.7 35.5 %copy-start.14 = (f32[128,512]{1,0:T(8,128)}, f32[128,512]{1,0:T(8,128)S(1)}, u32[]{:S(2)}) copy-start(f32[128,512]{1,0:T(8,128)S(1)} %slice.71) | copy-start | bytes 786436
  63.9 35.4 %copy-start.12 = (f32[128,512]{0,1:T(8,128)}, f32[128,512]{0,1:T(8,128)S(1)}, u32[]{:S(2)}) copy-start(f32[128,512]{0,1:T(8,128)S(1)} %copy.97) | copy-start | bytes 786436
  66.1 491.0 %all-gather.11.cloned.1.call-start = ((), (), s32[]{:S(2)}) async-start(), calls=%async_computation.7 | async-start | bytes 2359296 | tf_op jit(solution)/shard_map/all_gather | solution.py:163
  66.8 493.0 %all-gather.13.cloned.1.call-start = ((), (), s32[]{:S(2)}) async-start(), calls=%async_computation.8 | async-start | bytes 21233664 | tf_op jit(solution)/shard_map/all_gather | solution.py:164
  67.4 600.0 %reduce-scatter.6.cloned.1.call-start = ((), (), s32[]{:S(2)}) async-start(), calls=%async_computation.9 | async-start | bytes 2359296 | tf_op jit(solution)/shard_map/reduce_scatter | solution.py:251
  67.4 31.8 %collective-permute-start = (bf16[576,1024]{1,0:T(8,128)(2,1)S(1)}, bf16[576,1024]{1,0:T(8,128)(2,1)S(1)}, u32[]{:S(2)}, u32[]{:S(2)}) collective-permute-start(bf16[576,1024]{1,0:T(8,128)(2,1)S(1)} %copy-done.2), channel_id=1, source_target_pairs={{0,7},{1,0},{2,1},{3,2},{4,3},{5,4},{6,5},{7,6},{8,15},{9,8},{10,9... | collective-permute-start | bytes 3538952 | tf_op jit(solution)/shard_map/ppermute | solution.py:139
  99.2 73.7 %copy-start.3 = (bf16[576,1024]{1,0:T(8,128)(2,1)}, bf16[576,1024]{1,0:T(8,128)(2,1)S(1)}, u32[]{:S(2)}) copy-start(bf16[576,1024]{1,0:T(8,128)(2,1)S(1)} %collective-permute-done) | copy-start | bytes 3538948
  99.4 75.5 %copy-start.51 = (bf16[128]{0:T(256)(128)(2,1)S(1)}, bf16[128]{0:T(256)(128)(2,1)}, u32[]{:S(2)}) copy-start(bf16[128]{0:T(256)(128)(2,1)} %param.21) | copy-start | bytes 772
  99.5 71.0 %collective-permute-start.1 = (bf16[1152,1024]{1,0:T(8,128)(2,1)S(1)}, bf16[1152,1024]{1,0:T(8,128)(2,1)S(1)}, u32[]{:S(2)}, u32[]{:S(2)}) collective-permute-start(bf16[1152,1024]{1,0:T(8,128)(2,1)S(1)} %pad_maximum_fusion.1), channel_id=1, source_target_pairs={{0,6},{1,7},{2,0},{3,1},{4,2},{5,3},{6,4},{7,5},{8,14},{9,15},{10,... | collective-permute-start | bytes 7077896 | tf_op jit(solution)/shard_map/ppermute | solution.py:139
  172.9 356.9 %collective-permute-start.2 = (bf16[2304,1024]{1,0:T(8,128)(2,1)}, bf16[2304,1024]{1,0:T(8,128)(2,1)}, u32[]{:S(2)}, u32[]{:S(2)}) collective-permute-start(bf16[2304,1024]{1,0:T(8,128)(2,1)} %pad_maximum_fusion), channel_id=1, source_target_pairs={{0,4},{1,5},{2,6},{3,7},{4,0},{5,1},{6,2},{7,3},{8,12},{9,13},{10,... | collective-permute-start | bytes 14155784 | tf_op jit(solution)/shard_map/ppermute | solution.py:139
  363.7 6.0 copy-start.9
  377.0 159.0 %copy-start.4 = (bf16[576,1024]{1,0:T(8,128)(2,1)S(1)}, bf16[576,1024]{1,0:T(8,128)(2,1)}, u32[]{:S(2)}) copy-start(bf16[576,1024]{1,0:T(8,128)(2,1)} %copy-done.3) | copy-start | bytes 3538948
  543.8 6.0 copy-start.19
  543.8 6.0 copy-start.20
  543.8 6.0 copy-start.21
  559.2 29.6 %copy-start.41 = (f32[128]{0:T(128)}, f32[128]{0:T(128)S(1)}, u32[]{:S(2)}) copy-start(f32[128]{0:T(128)S(1)} %get-tuple-element.58) | copy-start | bytes 1540
  559.8 7.9 copy-start.16
  576.7 12.1 %copy-start.22 = (bf16[128,4608]{1,0:T(8,128)(2,1)}, bf16[128,4608]{1,0:T(8,128)(2,1)S(1)}, u32[]{:S(2)}) copy-start(bf16[128,4608]{1,0:T(8,128)(2,1)S(1)} %get-tuple-element.28) | copy-start | bytes 3538948
  576.7 12.1 %copy-start.23 = (bf16[128,4608]{1,0:T(8,128)(2,1)}, bf16[128,4608]{1,0:T(8,128)(2,1)S(1)}, u32[]{:S(2)}) copy-start(bf16[128,4608]{1,0:T(8,128)(2,1)S(1)} %get-tuple-element.29) | copy-start | bytes 3538948
  576.7 12.3 %copy-start.6 = (bf16[1024,1024]{1,0:T(8,128)(2,1)S(1)}, bf16[1024,1024]{1,0:T(8,128)(2,1)}, u32[]{:S(2)}) copy-start(bf16[1024,1024]{1,0:T(8,128)(2,1)} %all-gather.11.cloned.1.call-done) | copy-start | bytes 6291460
  591.8 6.5 copy-start.28
  591.8 6.5 copy-start.44
  616.1 88.0 %reduce-scatter.10.cloned.1.call-start = ((), (), s32[]{:S(2)}) async-start(), calls=%async_computation.11 | async-start | bytes 2359296 | tf_op jit(solution)/shard_map/reduce_scatter | solution.py:302
  618.2 137.3 %reduce-scatter.8.cloned.1.call-start = ((), (), s32[]{:S(2)}) async-start(), calls=%async_computation.10 | async-start | bytes 4718592 | tf_op jit(solution)/shard_map/reduce_scatter | solution.py:299
  625.9 5.9 copy-start.10
  625.9 46.1 %copy-start.13 = (f32[128,512]{0,1:T(8,128)S(1)}, f32[128,512]{0,1:T(8,128)}, u32[]{:S(2)}) copy-start(f32[128,512]{0,1:T(8,128)} %copy-done.12) | copy-start | bytes 786436
  681.7 174.0 %reduce-scatter.14.cloned.1.call-start = ((), (), s32[]{:S(2)}) async-start(), calls=%async_computation.13 | async-start | bytes 10616832 | tf_op jit(solution)/shard_map/reduce_scatter | solution.py:308
  688.4 356.0 %reduce-scatter.12.cloned.1.call-start = ((), (), s32[]{:S(2)}) async-start(), calls=%async_computation.12 | async-start | bytes 21233664 | tf_op jit(solution)/shard_map/reduce_scatter | solution.py:305
  699.9 345.8 %copy-start.39 = (f32[128,8]{0,1:T(8,128)S(1)}, f32[128,8]{0,1:T(8,128)}, u32[]{:S(2)}) copy-start(f32[128,8]{0,1:T(8,128)} %copy-done.37) | copy-start | bytes 12292
  699.9 346.0 %copy-start.15 = (f32[128,512]{1,0:T(8,128)S(1)}, f32[128,512]{1,0:T(8,128)}, u32[]{:S(2)}) copy-start(f32[128,512]{1,0:T(8,128)} %copy-done.14) | copy-start | bytes 786436
  699.9 347.0 %copy-start.11 = (f32[128,1024]{1,0:T(8,128)S(1)}, f32[128,1024]{1,0:T(8,128)}, u32[]{:S(2)}) copy-start(f32[128,1024]{1,0:T(8,128)} %slice.77) | copy-start | bytes 1572868
  699.9 452.4 %all-reduce.12.cloned.1.call-start = ((), (), s32[]{:S(2)}) async-start(), calls=%async_computation.14 | async-start | bytes 8650752 | tf_op jit(solution)/shard_map/psum | solution.py:325
  1052.3 8.0 copy-start.26
  1052.3 8.4 copy-start.18
  1052.4 8.8 copy-start.29
  1052.4 8.8 copy-start.46
  1060.3 32.5 %copy-start.50 = (f32[128]{0:T(128)S(1)}, f32[128]{0:T(128)}, u32[]{:S(2)}) copy-start(f32[128]{0:T(128)} %get-tuple-element.55) | copy-start | bytes 1540
  1152.4 6.2 copy-start.31
  1152.4 7.2 copy-start.36
  (21 other events, 67.3 us)
Sparse Core Ops, SparseCore 0:
  9.6 49.8 all-gather.6
  66.2 32.9 all-gather.8
  100.8 45.1 all-gather.10
  147.5 358.8 all-gather.12
  616.2 51.1 reduce-scatter.5
  669.6 34.4 reduce-scatter.9
  706.9 48.5 reduce-scatter.7
  757.8 97.8 reduce-scatter.13
  858.0 186.3 reduce-scatter.11
  1048.0 104.3 all-reduce.11
